TPU v7x, 32 devices: a whole 2x2x4 slice. The times are simulated.
32 devices in a mesh: row: 8 (over y, x, core), col: 4 (over z).
Axes of the slice: x: 2, y: 2, z: 4, core: 2. Of those that a mesh axis runs over, the one named last changes fastest.
Arguments:
- front_rows: bfloat16 [32, 128, 512], P('row', 'col'), may hold values from -0.109375 to 0.109375
- slot_blocks: int32 [32], P('row'), may hold values from -1 to 23, as said below
- inv_factor: float32 [512, 512], replicated
- ancestor_inv: float32 [3072, 3072], P('row', 'col'), may hold values from -6 to 6
Outputs:
- offdiag_inv: float32 [3072, 512], P(('row', 'col'))
- diag_inv: float32 [512, 512], P('col')
Inputs may be any that keep to these rules, and one draw needn't show every extreme that they name: `slot_blocks`: each of the 24 blocks stands in exactly one slot and -1 marks an empty slot. Block b belongs to column panel b // 6; the 4 slots of one row index hold at most 1 block of one panel, and some row index holds exactly 1 block of every panel.
All inputs are finite; a program needn't handle non-finite values.
Results may differ from a plain program's by a relative error of at most 0.0041.
Values may be sent and summed in bfloat16 or wider, within the bound.
A program may use at most 64 MiB of HBM per device.

v0:
```python
import jax
import jax.numpy as jnp
from jax import lax
from jax.sharding import PartitionSpec as P


def spread(block, axis, owner):
    block = jnp.where(lax.axis_index(axis) == owner, block, jnp.zeros_like(block))
    return lax.psum(block, axis)


def select_matrix(block_ids, panels, panel_blocks, cand_count):
    panel_of = jnp.where(block_ids >= 0, block_ids // panel_blocks, -1)
    member = panel_of[None, :] == panels[:, None]
    ranking = jnp.cumsum(member.astype(jnp.int32), axis=1) - 1
    levels = jnp.arange(cand_count, dtype=jnp.int32)
    return member[:, None, :] & (ranking[:, None, :] == levels[None, :, None])


def body(front_rows, slot_blocks, inv_factor, ancestor_inv):
    col_count = lax.axis_size("col")
    row_count = lax.axis_size("row")
    col_index = lax.axis_index("col")
    row_index = lax.axis_index("row")
    slot_count = front_rows.shape[0]
    block_height = front_rows.shape[1] * col_count
    panel_width = front_rows.shape[2]
    tile_rows, panel_rows = ancestor_inv.shape
    panel_blocks = panel_rows // block_height
    cand_count = slot_count // col_count
    own_panel = jnp.reshape(col_index, (1,))
    own_choice = select_matrix(slot_blocks, own_panel, panel_blocks, cand_count)[0]
    cand_ids = jnp.sum(jnp.where(own_choice, slot_blocks[None, :] + 1, 0), axis=1) - 1
    all_choice = select_matrix(
        slot_blocks, jnp.arange(col_count, dtype=jnp.int32), panel_blocks, cand_count
    )
    pieces_out = jnp.einsum(
        "pks,sbw->pkbw",
        all_choice.astype(jnp.bfloat16),
        front_rows,
        preferred_element_type=jnp.float32,
    ).astype(jnp.bfloat16)
    picked = lax.all_to_all(pieces_out, "col", split_axis=0, concat_axis=2, tiled=True)[0]
    scaled = jnp.einsum(
        "kbw,wv->kbv",
        picked.astype(jnp.float32),
        inv_factor,
        precision=lax.Precision.HIGHEST,
        preferred_element_type=jnp.float32,
    ).astype(jnp.bfloat16)

    def absorb(totals, one_block, offset, is_valid):
        partial_sum, assembled = totals
        clipped = jnp.clip(offset, 0, panel_blocks - 1) * block_height
        columns = lax.dynamic_slice_in_dim(ancestor_inv, clipped, block_height, 1)
        update = jnp.dot(
            columns,
            one_block.astype(jnp.float32),
            precision=lax.Precision.HIGHEST,
            preferred_element_type=jnp.float32,
        )
        partial_sum = partial_sum + jnp.where(is_valid, update, 0.0)
        current = lax.dynamic_slice_in_dim(assembled, clipped, block_height, 0)
        assembled = lax.dynamic_update_slice_in_dim(
            assembled, jnp.where(is_valid, one_block, current), clipped, 0
        )
        return (partial_sum, assembled)

    initial = (
        jnp.zeros((tile_rows, panel_width), jnp.float32),
        jnp.zeros((panel_rows, panel_width), jnp.bfloat16),
    )
    blocks = lax.all_gather(scaled, "row", axis=0, tiled=True)
    block_ids = lax.all_gather(cand_ids, "row", axis=0, tiled=True)

    def take_member(member_index, running):
        number = block_ids[member_index]
        offset = number - col_index * panel_blocks
        is_valid = (number >= 0) & (offset >= 0) & (offset < panel_blocks)
        one_block = lax.dynamic_index_in_dim(blocks, member_index, 0, keepdims=False)
        return absorb(running, one_block, offset, is_valid)

    partial_sum, assembled = lax.fori_loop(0, blocks.shape[0], take_member, initial)
    root_col = row_index * col_count // row_count
    panel_start = row_index * tile_rows - root_col * panel_rows
    own_rows = lax.dynamic_slice_in_dim(assembled, panel_start, tile_rows, 0)
    row_factor = spread(own_rows, "col", root_col)
    column_total = lax.psum_scatter(partial_sum, "col", scatter_dimension=0, tiled=True)
    share_rows = tile_rows // col_count
    own_factor = lax.dynamic_slice_in_dim(row_factor, col_index * share_rows, share_rows, 0)
    gram_part = jnp.einsum(
        "pi,pj->ij",
        own_factor.astype(jnp.float32),
        column_total,
        precision=lax.Precision.HIGHEST,
        preferred_element_type=jnp.float32,
    )
    diag_width = panel_width // col_count
    gram_piece = lax.psum_scatter(gram_part, "col", scatter_dimension=0, tiled=True)
    gram_block = lax.psum(gram_piece, "row")
    factor_cols = lax.dynamic_slice_in_dim(inv_factor, col_index * diag_width, diag_width, 1)
    factor_gram = jnp.einsum(
        "pi,pj->ij",
        factor_cols,
        inv_factor,
        precision=lax.Precision.HIGHEST,
        preferred_element_type=jnp.float32,
    )
    diag_rows = factor_gram + gram_block
    return (-column_total, diag_rows)


def solution(mesh):
    in_specs = (P("row", "col", None), P("row"), P(), P("row", "col"))
    out_specs = (P(("row", "col"), None), P("col", None))
    return jax.shard_map(body, mesh=mesh, in_specs=in_specs, out_specs=out_specs, check_vma=False)
```

profile of v0, /device:TPU:0, one launch (start us, length us, event | category | flops | bytes accessed | tf_op | source)
XLA Modules:
  0.0 238.0 jit_solution(14888302685680050499)
XLA Ops:
  7.3 0.7 fusion.22
  8.0 0.2 reduce_window_sum.18
  8.2 1.1 fusion.6
  9.3 12.2 %all_to_all.4 = bf16[4,1,32,512]{3,2,1,0:T(8,128)(2,1)S(1)} all-to-all(bf16[4,1,32,512]{3,2,1,0:T(8,128)(2,1)S(1)} %copy.10), channel_id=1, replica_groups=mesh['row'=8,'col'=4] {'col'}, dimensions={0} | all-to-all | bytes 262144 | tf_op jit(solution)/shard_map/all_to_all | solution.py:43
  21.6 1.2 convolution_convert_fusion.1
  22.7 0.0 all-reduce.4.cloned.1.call-start
  22.8 0.2 reduce-window.8
  23.0 0.6 fusion.23
  24.3 0.7 dynamic-slice
  24.9 0.8 dynamic-update-slice
  25.7 8.0 %all-reduce = s32[8]{0:T(128)S(1)} all-reduce(s32[8]{0:T(128)S(1)} %dynamic-update-slice), channel_id=1, replica_groups=mesh['row'=8,'col'=4] {'row'}, use_global_device_ids=true, to_apply=%add | all-reduce | flops 8 | bytes 64
  33.8 11.6 %all-gather.3.cloned.1.call-done = bf16[1024,512]{1,0:T(8,128)(2,1)} async-done(((bf16[128,512]{1,0:T(8,128)(2,1)}), bf16[1024,512]{1,0:T(8,128)(2,1)}) %all-gather.3.cloned.1.call-update) | async-done | bytes 1048592 | tf_op jit(solution)/shard_map/all_gather | solution.py:73
  45.4 0.1 broadcast_in_dim.33
  45.4 35.4 %while.18 = (s32[]{:T(128)}, f32[384,512]{1,0:T(8,128)S(1)}, bf16[768,512]{1,0:T(8,128)(2,1)S(1)}, s32[8]{0:T(128)S(1)}, s32[]{:T(128)}, /*index=5*/f32[384,768]...) while((s32[]{:T(128)}, f32[384,512]{1,0:T(8,128)S(1)}, ...), condition=%wide.region_4.5_spmd.clone, body=%wide.region_3.4_spmd.clone.sunk | while | flops 302645248 | bytes 2294048 | solution.py:83
  45.4 0.6 dynamic_slice.75
  47.3 1.5 fusion.35
  48.9 0.9 fusion.36
  49.9 0.6 dynamic_slice.75
  51.8 1.6 fusion.35
  53.3 0.9 fusion.36
  54.3 0.6 dynamic_slice.75
  56.2 1.5 fusion.35
  57.7 0.9 fusion.36
  58.7 0.6 dynamic_slice.75
  60.6 1.5 fusion.35
  62.2 0.9 fusion.36
  63.1 0.6 dynamic_slice.75
  65.0 1.6 fusion.35
  66.6 0.9 fusion.36
  67.6 0.6 dynamic_slice.75
  69.5 1.5 fusion.35
  71.0 0.9 fusion.36
  72.0 0.6 dynamic_slice.75
  73.9 1.5 fusion.35
  75.4 0.9 fusion.36
  76.4 0.6 dynamic_slice.75
  78.3 1.6 fusion.35
  79.9 0.9 fusion.36
  80.8 0.9 dynamic-slice_select_fusion
  81.8 0.7 reduce-scatter.3.cloned.1.call-update
  82.6 36.3 %all-reduce.4.cloned.1.call-done = bf16[384,512]{1,0:T(8,128)(2,1)} async-done(((bf16[384,512]{1,0:T(8,128)(2,1)}), bf16[384,512]{1,0:T(8,128)(2,1)}) %all-reduce.4.cloned.1.call-update) | async-done | bytes 393232 | tf_op jit(solution)/shard_map/psum | solution.py:9
  118.9 25.2 %reduce-scatter.3.cloned.1.call-done = f32[96,512]{1,0:T(8,128)} async-done(((f32[384,512]{1,0:T(8,128)}), f32[96,512]{1,0:T(8,128)}) %reduce-scatter.3.cloned.1.call-update) | async-done | bytes 196624 | tf_op jit(solution)/shard_map/reduce_scatter | solution.py:88
  144.1 2.6 %fusion.9 = f32[512,512]{1,0:T(8,128)} fusion(f32[96,512]{1,0:T(8,128)} %reduce-scatter.3.cloned.1.call-done, bf16[384,512]{1,0:T(8,128)(2,1)} %all-reduce.4.cloned.1.call-done, s32[]{:T(128)S(6)} %select_n.106), kind=kOutput, calls=%fused_computation.15 | convolution fusion | flops 301989888 | bytes 1343492 | tf_op jit(solution)/shard_map/pi,pj->ij/dot_general | solution.py:91
  146.8 0.0 all-reduce.6.cloned.1.call-start
  146.8 26.9 %reduce-scatter.5.cloned.1.call-done = f32[128,512]{1,0:T(8,128)} async-done(((f32[512,512]{1,0:T(8,128)}), f32[128,512]{1,0:T(8,128)}) %reduce-scatter.5.cloned.1.call-update) | async-done | bytes 262160 | tf_op jit(solution)/shard_map/reduce_scatter | solution.py:99
  173.8 0.7 neg.3
  174.5 54.6 %all-reduce.6.cloned.1.call-done = f32[128,512]{1,0:T(8,128)} async-done(((f32[128,512]{1,0:T(8,128)}), f32[128,512]{1,0:T(8,128)}) %all-reduce.6.cloned.1.call-update) | async-done | bytes 262160 | tf_op jit(solution)/shard_map/psum | solution.py:100
  229.1 2.4 %convolution_add_fusion = f32[128,512]{1,0:T(8,128)} fusion(f32[128,512]{1,0:T(8,128)} %all-reduce.6.cloned.1.call-done, f32[512,512]{1,0:T(8,128)S(1)} %copy-done, s32[]{:T(128)S(6)} %select_n.101), kind=kOutput, calls=%fused_computation.8 | convolution fusion | flops 402718720 | bytes 1835012 | tf_op jit(solution)/shard_map/pi,pj->ij/dot_general | solution.py:102
  (21 shorter events, 0.3 us)
Async XLA Ops:
  7.2 14.4 %copy-start = (f32[512,512]{1,0:T(8,128)S(1)}, f32[512,512]{1,0:T(8,128)}, u32[]{:S(2)}) copy-start(f32[512,512]{1,0:T(8,128)} %param.8) | copy-start | bytes 3145732
  7.2 17.1 %copy-start.4 = (u32[32]{0:T(128)S(1)}, u32[32]{0:T(128)}, u32[]{:S(2)}) copy-start(u32[32]{0:T(128)} %constant.149) | copy-start | bytes 388
  7.2 15.8 %copy-start.3 = (s32[4]{0:T(128)S(1)}, s32[4]{0:T(128)}, u32[]{:S(2)}) copy-start(s32[4]{0:T(128)} %param.7) | copy-start | bytes 52
  7.2 38.2 %all-gather.3.cloned.1.call-start = ((), (), s32[]{:S(2)}) async-start(), calls=%async_computation.7 | async-start | bytes 1179648 | tf_op jit(solution)/shard_map/all_gather | solution.py:73
  22.7 96.1 %all-reduce.4.cloned.1.call-start = ((), (), s32[]{:S(2)}) async-start(), calls=%async_computation.4 | async-start | bytes 786432 | tf_op jit(solution)/shard_map/psum | solution.py:9
  80.8 1.0 copy-start.1
  81.8 62.4 %reduce-scatter.3.cloned.1.call-start = ((), (), s32[]{:S(2)}) async-start(), calls=%async_computation.3 | async-start | bytes 983040 | tf_op jit(solution)/shard_map/reduce_scatter | solution.py:88
  82.5 91.2 %reduce-scatter.5.cloned.1.call-start = ((), (), s32[]{:S(2)}) async-start(), calls=%async_computation.5 | async-start | bytes 1310720 | tf_op jit(solution)/shard_map/reduce_scatter | solution.py:99
  144.1 29.6 %copy-start.2 = (f32[96,512]{1,0:T(8,128)S(1)}, f32[96,512]{1,0:T(8,128)}, u32[]{:S(2)}) copy-start(f32[96,512]{1,0:T(8,128)} %reduce-scatter.3.cloned.1.call-done) | copy-start | bytes 589828
  146.8 82.3 %all-reduce.6.cloned.1.call-start = ((), (), s32[]{:S(2)}) async-start(), calls=%async_computation.6 | async-start | bytes 524288 | tf_op jit(solution)/shard_map/psum | solution.py:100
Sparse Core Ops, SparseCore 0:
  22.9 22.4 all-gather.2
  81.9 36.9 all-reduce.3
  121.2 22.8 reduce-scatter.2
  146.9 26.7 reduce-scatter.4
  176.6 52.3 all-reduce.5
where the time goes:
time: 239 us; the launch traced here: 238 us
  waiting for transfers between devices  155 us (65%)
  blocking collectives  20.2 us (8%)
  matrix products  19.7 us (8%)
  between operations  14.5 us (6%)
  other arithmetic  10.9 us (5%)
  loops' own time  10.7 us (4%)
  local copies, waits for them, and re-layouts  6.3 us (3%)
    psum x1, waiting for transfers between devices, body(): gram_block = lax.psum(gram_piece, 'row')  54.6 us
    psum x1, waiting for transfers between devices, spread(): return lax.psum(block, axis)  36.3 us
    reduce_scatter x1, waiting for transfers between devices, body(): lax.psum_scatter(gram_part, 'col', scatter_dimension=0, tiled=True)  26.9 us
    reduce_scatter x1, waiting for transfers between devices, body(): lax.psum_scatter(partial_sum, 'col', scatter_dimension=0, tiled=True)  25.2 us
    dot_general x8, matrix products, absorb(): jnp.dot(columns, one_block.astype(jnp.float32), precision=lax.Precision.H...  12.4 us
    all_to_all x1, blocking collectives, body(): lax.all_to_all(pieces_out, 'col', split_axis=0, concat_axis=2, tiled=True)  12.2 us
    all_gather x1, waiting for transfers between devices, body(): blocks = lax.all_gather(scaled, 'row', axis=0, tiled=True)  11.6 us
    another operation x1, loops' own time, body(): lax.fori_loop(0, blocks.shape[0], take_member, initial)  10.7 us
  transfers between devices with their start and end apart: 5, of which 5 were waited for; matrix products, arithmetic and copies ran while one was open for 1% of the time, Pallas kernels for 0%

commit v1 on v0

v1 whole, which is shorter than its diff:
```python
import functools

import jax
import jax.numpy as jnp
from jax import lax
from jax.experimental import pallas as pl
from jax.experimental.pallas import tpu as pltpu
from jax.sharding import PartitionSpec as P

MESH = pl.DeviceIdType.MESH
F32 = jnp.float32
BF16 = jnp.bfloat16


def split(x):
    high = x.astype(BF16)
    return high, (x - high.astype(F32)).astype(BF16)


def dot(a, b):
    return jnp.dot(a, b, preferred_element_type=F32)


def tdot(a, b):
    return lax.dot_general(a, b, (((0,), (0,)), ((), ())), preferred_element_type=F32)


def kernel(
    n_row, n_col, front, slots, factor_hbm, anc_hbm, out, diag,
    factor, anc, ids, pieces, blocks, perm, acc, part, part_in, own_rows, spread,
    gram, fgram, row_out, row_in, col_out, col_in, total_out, total_in,
    load_sem, ids_s, ids_r, a_s, a_r, b_s, b_r, f_s, c_s, c_r, w_s, w_r,
    gr_s, gr_r, gc_s, gc_r, gg_s, gg_r, gf_s,
):
    row = lax.axis_index("row")
    col = lax.axis_index("col")
    slot_count, height, width = front.shape
    block_height = height * n_col
    tile_rows, panel_rows = anc.shape
    panel_blocks = panel_rows // block_height
    share = tile_rows // n_col
    piece = row_out.shape[2]
    partner = row + 1 - 2 * lax.rem(row, 2)

    def row_peer(step):
        return lax.rem(row + step, n_row)

    def col_peer(step):
        return lax.rem(col + step, n_col)

    def copy(src, dst, s_sem, r_sem, to_row, to_col):
        return pltpu.make_async_remote_copy(
            src_ref=src, dst_ref=dst, send_sem=s_sem, recv_sem=r_sem,
            device_id=(to_row, to_col), device_id_type=MESH,
        )

    barrier = pltpu.get_barrier_semaphore()
    for step in range(1, n_row):
        pl.semaphore_signal(barrier, inc=1, device_id=(row_peer(step), col), device_id_type=MESH)
    for step in range(1, n_col):
        pl.semaphore_signal(barrier, inc=1, device_id=(row, col_peer(step)), device_id_type=MESH)
    load_factor = pltpu.make_async_copy(factor_hbm, factor, load_sem.at[0])
    load_anc = pltpu.make_async_copy(anc_hbm, anc, load_sem.at[1])
    load_factor.start()
    load_anc.start()

    number = jnp.int32(0)
    for s in range(slot_count):
        local = slots[s] - col * panel_blocks
        number = number + jnp.where((local >= 0) & (local < panel_blocks), local + 1, 0)
    ids[row] = jnp.full(ids.shape[1:], number - 1, jnp.int32)

    picked = []
    rows_in = [front[s].astype(F32) for s in range(slot_count)]
    for p in range(n_col):
        chosen = jnp.zeros((height, width), F32)
        for s in range(slot_count):
            local = slots[s] - p * panel_blocks
            keep = jnp.where((local >= 0) & (local < panel_blocks), 1.0, 0.0)
            chosen = chosen + rows_in[s] * keep
        picked.append(chosen)
    picked = jnp.concatenate(picked, axis=0).astype(BF16)
    load_factor.wait()
    f_high, f_low = split(factor[...])
    scaled = dot(picked, f_high) + dot(picked, f_low)
    for p in range(n_col):
        pieces[p] = scaled[p * height:(p + 1) * height].astype(BF16)
    blocks[row, col] = pieces[col]
    pl.semaphore_wait(barrier, n_row + n_col - 2)

    def a_copy(peer, there):
        return copy(pieces.at[peer], blocks.at[row, there], a_s.at[peer], a_r.at[there], row, peer)

    for step in range(1, n_col):
        a_copy(col_peer(step), col).start()

    def id_copy(peer, there):
        return copy(ids.at[there], ids.at[there], ids_s.at[peer], ids_r.at[there], peer, col)

    for step in range(1, n_row):
        id_copy(row_peer(step), row).start()
    load_anc.wait()
    for step in range(1, n_row):
        id_copy(row_peer(step), row_peer(step)).wait_recv()
    for step in range(1, n_col):
        a_copy(col_peer(step), col_peer(step)).wait_recv()

    def b_copy(peer, there):
        return copy(blocks.at[there], blocks.at[there], b_s.at[peer], b_r.at[there], peer, col)

    def b_forward(there):
        return copy(blocks.at[there], blocks.at[there], f_s.at[there], b_r.at[there], partner, col)

    for step in range(2, n_row, 2):
        b_copy(row_peer(step), row).start()
    b_copy(partner, row).start()

    @pl.loop(0, n_row)
    def _(m):
        mask_ids = ids[m, 0:1, 0:block_height]
        total = jnp.zeros((tile_rows, block_height), F32)
        for b in range(panel_blocks):
            keep = jnp.where(mask_ids == b, 1.0, 0.0)
            total = total + anc[:, b * block_height:(b + 1) * block_height] * keep
        perm[m] = total.astype(BF16)

    def block_of(m):
        if height % 16 == 0:
            return blocks[m].reshape(block_height, width)
        return blocks[m].astype(F32).reshape(block_height, width).astype(BF16)

    acc[...] = dot(perm[row], block_of(row))
    f_high, f_low = split(factor[...])
    fgram[...] = tdot(f_high, f_high) + tdot(f_high, f_low) + tdot(f_low, f_high)
    for step in range(2, n_row, 2):
        m = row_peer(n_row - step)
        b_copy(m, m).wait_recv()
        b_forward(m).start()
        acc[...] += dot(perm[m], block_of(m))
    for step in range(0, n_row, 2):
        m = lax.rem(partner + n_row - step, n_row)
        b_copy(m, m).wait_recv()
        acc[...] += dot(perm[m], block_of(m))

    for p in range(n_col):
        part[p] = acc[p * share:(p + 1) * share, :].astype(BF16)

    def c_copy(peer, there):
        return copy(part.at[peer], part_in.at[there], c_s.at[peer], c_r.at[there], row, peer)

    for step in range(1, n_col):
        c_copy(col_peer(step), col).start()

    root = row * n_col // n_row
    first = (row * tile_rows - root * panel_rows) // block_height

    def w_copy(peer):
        return copy(spread.at[peer], own_rows, w_s.at[peer], w_r.at[0], row, peer)

    @pl.when(col == root)
    def _():
        rows = []
        for i in range(tile_rows // block_height):
            chosen = jnp.zeros((block_height, width), F32)
            for m in range(n_row):
                keep = jnp.where(ids[m, 0:1, :] == first + i, 1.0, 0.0)
                chosen = chosen + block_of(m).astype(F32) * keep
            rows.append(chosen)
        rows = jnp.concatenate(rows, axis=0)
        for p in range(n_col):
            spread[p] = rows[p * share:(p + 1) * share].astype(BF16)
        for step in range(1, n_col):
            w_copy(col_peer(step)).start()
        own_rows[...] = spread[col]

    total = acc[pl.ds(pl.multiple_of(col * share, 8), share), :]
    for step in range(1, n_col):
        m = col_peer(step)
        c_copy(m, m).wait_recv()
        total = total + part_in[m].astype(F32)
    out[...] = -total

    @pl.when(col != root)
    def _():
        w_copy(root).wait_recv()

    t_high, t_low = split(total)
    mine = own_rows[...]
    gram[...] = tdot(mine, t_high) + tdot(mine, t_low)
    for j in range(n_row):
        for p in range(n_col):
            start = (p * n_row + j) * piece
            row_out[j, p] = gram[start:start + piece, :].astype(row_out.dtype)

    def gr_copy(peer, there):
        return copy(row_out.at[peer], row_in.at[there], gr_s.at[peer], gr_r.at[there], peer, col)

    for step in range(1, n_row):
        gr_copy(row_peer(step), row).start()
    summed = row_out[row].astype(F32)
    for step in range(1, n_row):
        m = row_peer(n_row - step)
        gr_copy(m, m).wait_recv()
        summed = summed + row_in[m].astype(F32)
    col_out[...] = summed

    def gc_copy(peer, there):
        return copy(col_out.at[peer], col_in.at[there], gc_s.at[peer], gc_r.at[there], row, peer)

    for step in range(1, n_col):
        gc_copy(col_peer(step), col).start()
    final = col_out[col]
    for step in range(1, n_col):
        m = col_peer(n_col - step)
        gc_copy(m, m).wait_recv()
        final = final + col_in[m]
    total_in[row] = final

    def gg_copy(peer, there):
        return copy(total_in.at[there], total_in.at[there], gg_s.at[peer], gg_r.at[there], peer, col)

    for step in range(1, n_row):
        gg_copy(row_peer(step), row).start()
    for step in range(1, n_row):
        m = row_peer(n_row - step)
        gg_copy(m, m).wait_recv()
    width_out = diag.shape[0]
    gathered = jnp.concatenate([total_in[m] for m in range(n_row)], axis=0)
    diag[...] = gathered + fgram[pl.ds(pl.multiple_of(col * width_out, 8), width_out), :]

    for step in range(1, n_col):
        peer = col_peer(step)
        a_copy(peer, col).wait_send()
        c_copy(peer, col).wait_send()
        gc_copy(peer, col).wait_send()
    for step in range(1, n_row):
        peer = row_peer(step)
        id_copy(peer, row).wait_send()
        gr_copy(peer, row).wait_send()
        gg_copy(peer, row).wait_send()
    for step in range(2, n_row, 2):
        b_copy(row_peer(step), row).wait_send()
        b_forward(row_peer(n_row - step)).wait_send()
    b_copy(partner, row).wait_send()

    @pl.when(col == root)
    def _():
        for step in range(1, n_col):
            w_copy(col_peer(step)).wait_send()


def solution(mesh):
    n_row, n_col = mesh.shape["row"], mesh.shape["col"]

    def body(front_rows, slot_blocks, inv_factor, ancestor_inv):
        _, height, width = front_rows.shape
        tile_rows, panel_rows = ancestor_inv.shape
        block_height = height * n_col
        share = tile_rows // n_col
        diag_width = width // n_col
        piece = diag_width // n_row
        wire = BF16 if piece % 16 == 0 else F32
        vmem = pltpu.VMEM
        dma = pltpu.SemaphoreType.DMA
        return pl.pallas_call(
            functools.partial(kernel, n_row, n_col),
            out_shape=(
                jax.ShapeDtypeStruct((share, width), F32),
                jax.ShapeDtypeStruct((diag_width, width), F32),
            ),
            in_specs=[
                pl.BlockSpec(memory_space=pltpu.VMEM),
                pl.BlockSpec(memory_space=pltpu.SMEM),
                pl.BlockSpec(memory_space=pl.ANY),
                pl.BlockSpec(memory_space=pl.ANY),
            ],
            out_specs=(
                pl.BlockSpec(memory_space=pltpu.VMEM),
                pl.BlockSpec(memory_space=pltpu.VMEM),
            ),
            scratch_shapes=[
                vmem((width, width), F32),
                vmem((tile_rows, panel_rows), F32),
                vmem((n_row, 8, width), jnp.int32),
                vmem((n_col, height, width), BF16),
                vmem((n_row, n_col, height, width), BF16),
                vmem((n_row, tile_rows, block_height), BF16),
                vmem((tile_rows, width), F32),
                vmem((n_col, share, width), BF16),
                vmem((n_col, share, width), BF16),
                vmem((share, width), BF16),
                vmem((n_col, share, width), BF16),
                vmem((width, width), F32),
                vmem((width, width), F32),
                vmem((n_row, n_col, piece, width), wire),
                vmem((n_row, n_col, piece, width), wire),
                vmem((n_col, piece, width), F32),
                vmem((n_col, piece, width), F32),
                vmem((n_row, piece, width), F32),
                vmem((n_row, piece, width), F32),
                dma((2,)),
                dma((n_row,)), dma((n_row,)),
                dma((n_col,)), dma((n_col,)),
                dma((n_row,)), dma((n_row,)), dma((n_row,)),
                dma((n_col,)), dma((n_col,)),
                dma((n_col,)), dma((1,)),
                dma((n_row,)), dma((n_row,)),
                dma((n_col,)), dma((n_col,)),
                dma((n_row,)), dma((n_row,)), dma((n_row,)),
            ],
            compiler_params=pltpu.CompilerParams(
                collective_id=0, has_side_effects=True, vmem_limit_bytes=60 * 1024 * 1024
            ),
        )(front_rows, slot_blocks, inv_factor, ancestor_inv)

    in_specs = (P("row", "col", None), P("row"), P(), P("row", "col"))
    out_specs = (P(("row", "col"), None), P("col", None))
    return jax.shard_map(body, mesh=mesh, in_specs=in_specs, out_specs=out_specs, check_vma=False)
```

time: 239 us -> 56.5 us (0.24)
  waiting for transfers between devices: 155 us -> 0 us
  Pallas kernels: 0 us -> 52.3 us
  blocking collectives: 20.2 us -> 0 us
  matrix products: 19.7 us -> 0 us
  between operations: 14.5 us -> 0.64 us
  other arithmetic: 10.9 us -> 0 us
  loops' own time: 10.7 us -> 0 us
  local copies, waits for them, and re-layouts: 6.3 us -> 3.29 us
    psum x2 -> x0, waiting for transfers between devices: 90.9 us -> none  [the longest x1 54.6 us: body(): gram_block = lax.psum(gram_piece, 'row')]
    pallas_call x0 -> x1, Pallas kernels: none -> 52.3 us  [body(): pl.pallas_call(functools.partial(kernel, n_row, n_col), out_shape=(jax.Sh...]
    reduce_scatter x2 -> x0, waiting for transfers between devices: 52.2 us -> none  [the longest x1 26.9 us: body(): lax.psum_scatter(gram_part, 'col', scatter_dimension=0, tiled=True)]
    dot_general x12 -> x0, matrix products: 19.7 us -> none  [the longest x8 12.4 us: absorb(): jnp.dot(columns, one_block.astype(jnp.float32), precision=lax.Precision.H...]
    all_to_all x1 -> x0, blocking collectives: 12.2 us -> none  [body(): lax.all_to_all(pieces_out, 'col', split_axis=0, concat_axis=2, tiled=True)]
    all_gather x1 -> x0, waiting for transfers between devices: 11.6 us -> none  [body(): blocks = lax.all_gather(scaled, 'row', axis=0, tiled=True)]
    another operation x1 -> x0, loops' own time: 10.7 us -> none  [body(): lax.fori_loop(0, blocks.shape[0], take_member, initial)]
    unnamed x1 -> x0, blocking collectives: 8.02 us -> none
  transfers between devices with their start and end apart: 5 -> 0, of which waited for: 5 -> 0; matrix products, arithmetic and copies ran while one was open for 1% -> 0% of each run, Pallas kernels for 0% -> 0%
where the time goes in v1:
time: 56.5 us; the launch traced here: 56.2 us
  Pallas kernels  52.3 us (93%)
  local copies, waits for them, and re-layouts  3.29 us (6%)
  between operations  0.64 us (1%)
    pallas_call x1, Pallas kernels, body(): pl.pallas_call(functools.partial(kernel, n_row, n_col), out_shape=(jax.Sh...  52.3 us
    unnamed x2, local copies, waits for them, and re-layouts  3.29 us

profile of v1, /device:TPU:0, one launch (start us, length us, event | category | flops | bytes accessed | tf_op | source)
XLA Modules:
  0.0 56.2 jit_solution(14248739824993817481)
XLA Ops:
  0.6 52.3 %shard_map.59 = (f32[96,512]{1,0:T(8,128)}, f32[128,512]{1,0:T(8,128)}) custom-call(bf16[4,32,512]{2,1,0:T(8,128)(2,1)} %front.1, s32[4]{0:T(128)} %slots.1, f32[512,512]{1,0:T(8,128)} %factor_hbm.1, f32[384,768]{1,0:T(8,128)} %anc_hbm.1), custom_call_target="tpu_custom_call" | custom-call | tf_op jit(solution)/shard_map/pallas_call | solution.py:265
  52.9 1.6 %copy.8 = f32[96,512]{1,0:T(8,128)} copy(f32[96,512]{1,0:T(8,128)} %get-tuple-element.4) | data formatting | bytes 393216
  54.5 1.7 %copy.9 = f32[128,512]{1,0:T(8,128)} copy(f32[128,512]{1,0:T(8,128)} %get-tuple-element.5) | data formatting | bytes 524288

commit v2 on v1

v2 whole, which is shorter than its diff:
```python
import functools

import jax
import jax.numpy as jnp
from jax import lax
from jax.experimental import pallas as pl
from jax.experimental.pallas import tpu as pltpu
from jax.sharding import PartitionSpec as P

MESH = pl.DeviceIdType.MESH
F32 = jnp.float32
BF16 = jnp.bfloat16


def split(x):
    high = x.astype(BF16)
    return high, (x - high.astype(F32)).astype(BF16)


def dot(a, b):
    return jnp.dot(a, b, preferred_element_type=F32)


def tdot(a, b):
    return lax.dot_general(a, b, (((0,), (0,)), ((), ())), preferred_element_type=F32)


def kernel(
    n_row, n_col, parts, front, slots, factor_hbm, anc_hbm, out, diag, fdiag,
    factor, anc, ids, pieces, blocks, perm, acc, part, part_in, own_rows, spread,
    gram, row_out, row_in, col_out, col_in, total_in,
    load_sem, ids_s, ids_r, a_s, a_r, b_s, b_r, f_s, c_s, c_r, w_s, w_r,
    gr_s, gr_r, gc_s, gc_r, gg_s, gg_r,
):
    row = lax.axis_index("row")
    col = lax.axis_index("col")
    slot_count, height, width = front.shape
    block_height = height * n_col
    tile_rows, panel_rows = anc.shape
    panel_blocks = panel_rows // block_height
    share = tile_rows // n_col
    piece = row_out.shape[3]
    part_width = width // parts
    partner = row + 1 - 2 * lax.rem(row, 2)

    def row_peer(step):
        return lax.rem(row + step, n_row)

    def col_peer(step):
        return lax.rem(col + step, n_col)

    def copy(src, dst, s_sem, r_sem, to_row, to_col):
        return pltpu.make_async_remote_copy(
            src_ref=src, dst_ref=dst, send_sem=s_sem, recv_sem=r_sem,
            device_id=(to_row, to_col), device_id_type=MESH,
        )

    barrier = pltpu.get_barrier_semaphore()
    for step in range(1, n_row):
        pl.semaphore_signal(barrier, inc=1, device_id=(row_peer(step), col), device_id_type=MESH)
    for step in range(1, n_col):
        pl.semaphore_signal(barrier, inc=1, device_id=(row, col_peer(step)), device_id_type=MESH)
    load_factor = pltpu.make_async_copy(factor_hbm, factor, load_sem.at[0])
    load_anc = pltpu.make_async_copy(anc_hbm, anc, load_sem.at[1])
    load_factor.start()
    load_anc.start()

    number = jnp.int32(0)
    for s in range(slot_count):
        local = slots[s] - col * panel_blocks
        number = number + jnp.where((local >= 0) & (local < panel_blocks), local + 1, 0)
    ids[row] = jnp.full(ids.shape[1:], number - 1, jnp.int32)

    picked = []
    rows_in = [front[s].astype(F32) for s in range(slot_count)]
    for p in range(n_col):
        chosen = jnp.zeros((height, width), F32)
        for s in range(slot_count):
            local = slots[s] - p * panel_blocks
            keep = jnp.where((local >= 0) & (local < panel_blocks), 1.0, 0.0)
            chosen = chosen + rows_in[s] * keep
        picked.append(chosen)
    picked = jnp.concatenate(picked, axis=0).astype(BF16)
    load_factor.wait()
    f_high, f_low = split(factor[...])
    scaled = dot(picked, f_high) + dot(picked, f_low)
    for h in range(parts):
        for p in range(n_col):
            piece_rows = scaled[p * height:(p + 1) * height, h * part_width:(h + 1) * part_width]
            pieces[h, p] = piece_rows.astype(BF16)
        blocks[h, row, col] = pieces[h, col]
    pl.semaphore_wait(barrier, n_row + n_col - 2)

    def a_copy(h, peer, there):
        return copy(
            pieces.at[h, peer], blocks.at[h, row, there], a_s.at[h, peer], a_r.at[h, there], row, peer
        )

    def id_copy(peer, there):
        return copy(ids.at[there], ids.at[there], ids_s.at[peer], ids_r.at[there], peer, col)

    for h in range(parts):
        for step in range(1, n_col):
            a_copy(h, col_peer(step), col).start()
        if h == 0:
            for step in range(1, n_row):
                id_copy(row_peer(step), row).start()

    def b_copy(h, peer, there):
        return copy(
            blocks.at[h, there], blocks.at[h, there], b_s.at[h, peer], b_r.at[h, there], peer, col
        )

    def b_forward(h, there):
        return copy(
            blocks.at[h, there], blocks.at[h, there], f_s.at[h, there], b_r.at[h, there], partner, col
        )

    for h in range(parts):
        for step in range(1, n_col):
            a_copy(h, col_peer(step), col_peer(step)).wait_recv()
        for step in range(2, n_row, 2):
            b_copy(h, row_peer(step), row).start()
        b_copy(h, partner, row).start()

    for step in range(1, n_row):
        id_copy(row_peer(step), row_peer(step)).wait_recv()
    load_anc.wait()

    @pl.loop(0, n_row)
    def _(m):
        mask_ids = ids[m, 0:1, 0:block_height]
        total = jnp.zeros((tile_rows, block_height), F32)
        for b in range(panel_blocks):
            keep = jnp.where(mask_ids == b, 1.0, 0.0)
            total = total + anc[:, b * block_height:(b + 1) * block_height] * keep
        perm[m] = total.astype(BF16)

    def block_of(h, m):
        if height % 16 == 0:
            return blocks[h, m].reshape(block_height, part_width)
        return blocks[h, m].astype(F32).reshape(block_height, part_width).astype(BF16)

    root = row * n_col // n_row
    first = (row * tile_rows - root * panel_rows) // block_height

    def c_copy(h, peer, there):
        return copy(
            part.at[h, peer], part_in.at[h, there], c_s.at[h, peer], c_r.at[h, there], row, peer
        )

    def w_copy(h, peer):
        return copy(spread.at[h, peer], own_rows.at[h], w_s.at[h, peer], w_r.at[h], row, peer)

    def send_sums(h):
        for p in range(n_col):
            part[h, p] = acc[h, p * share:(p + 1) * share, :].astype(BF16)
        for step in range(1, n_col):
            c_copy(h, col_peer(n_col - step), col).start()

    def send_rows(h):
        @pl.when(col == root)
        def _():
            rows = []
            for i in range(tile_rows // block_height):
                chosen = jnp.zeros((block_height, part_width), F32)
                for m in range(n_row):
                    keep = jnp.where(ids[m, 0:1, 0:part_width] == first + i, 1.0, 0.0)
                    chosen = chosen + block_of(h, m).astype(F32) * keep
                rows.append(chosen)
            rows = jnp.concatenate(rows, axis=0)
            for p in range(n_col):
                spread[h, p] = rows[p * share:(p + 1) * share].astype(BF16)
            for step in range(1, n_col):
                w_copy(h, col_peer(step)).start()
            own_rows[h] = spread[h, col]

    for h in range(parts):
        acc[h] = dot(perm[row], block_of(h, row))
        for step in range(2, n_row, 2):
            m = row_peer(n_row - step)
            b_copy(h, m, m).wait_recv()
            b_forward(h, m).start()
            acc[h] += dot(perm[m], block_of(h, m))
        for step in range(0, n_row, 2):
            m = lax.rem(partner + n_row - step, n_row)
            b_copy(h, m, m).wait_recv()
            acc[h] += dot(perm[m], block_of(h, m))
        if h < parts - 1:
            send_sums(h)
            send_rows(h)
        else:
            send_rows(h)
            send_sums(h)

    f_high, f_low = split(factor[...])
    gram[...] = tdot(f_high, f_high) + tdot(f_high, f_low) + tdot(f_low, f_high)
    width_out = diag.shape[0]
    fdiag[...] = gram[pl.ds(pl.multiple_of(col * width_out, 8), width_out), :]

    def gr_copy(h, peer, there):
        return copy(
            row_out.at[h, peer], row_in.at[h, there], gr_s.at[h, peer], gr_r.at[h, there], peer, col
        )

    def gc_copy(h, peer, there):
        return copy(
            col_out.at[h, peer], col_in.at[h, there], gc_s.at[h, peer], gc_r.at[h, there], row, peer
        )

    def gg_copy(h, peer, there):
        return copy(
            total_in.at[h, there], total_in.at[h, there], gg_s.at[h, peer], gg_r.at[h, there], peer, col
        )

    for h in range(parts):
        lanes = slice(h * part_width, (h + 1) * part_width)
        total = acc[h, pl.ds(pl.multiple_of(col * share, 8), share), :]
        for step in range(1, n_col):
            m = col_peer(step)
            c_copy(h, m, m).wait_recv()
            total = total + part_in[h, m].astype(F32)
        out[:, lanes] = total
        t_high, t_low = split(total)
        for g in range(parts):
            if h == 0:
                @pl.when(col != root)
                def _():
                    w_copy(g, root).wait_recv()
            mine = own_rows[g]
            rows_g = slice(g * part_width, (g + 1) * part_width)
            gram[rows_g, lanes] = tdot(mine, t_high) + tdot(mine, t_low)
        for j in range(n_row):
            for p in range(n_col):
                start = (p * n_row + j) * piece
                row_out[h, j, p] = gram[start:start + piece, lanes].astype(row_out.dtype)
        for step in range(1, n_row):
            gr_copy(h, row_peer(step), row).start()

    for h in range(parts):
        summed = row_out[h, row].astype(F32)
        for step in range(1, n_row):
            m = row_peer(n_row - step)
            gr_copy(h, m, m).wait_recv()
            summed = summed + row_in[h, m].astype(F32)
        col_out[h] = summed
        for step in range(1, n_col):
            gc_copy(h, col_peer(step), col).start()

    for h in range(parts):
        final = col_out[h, col]
        for step in range(1, n_col):
            m = col_peer(n_col - step)
            gc_copy(h, m, m).wait_recv()
            final = final + col_in[h, m]
        total_in[h, row] = final
        for step in range(1, n_row):
            gg_copy(h, row_peer(step), row).start()

    for h in range(parts):
        for step in range(1, n_row):
            m = row_peer(n_row - step)
            gg_copy(h, m, m).wait_recv()
        gathered = jnp.concatenate([total_in[h, m] for m in range(n_row)], axis=0)
        diag[:, h * part_width:(h + 1) * part_width] = gathered

    for h in range(parts):
        for step in range(1, n_col):
            peer = col_peer(step)
            a_copy(h, peer, col).wait_send()
            c_copy(h, peer, col).wait_send()
            gc_copy(h, peer, col).wait_send()
        for step in range(1, n_row):
            peer = row_peer(step)
            if h == 0:
                id_copy(peer, row).wait_send()
            gr_copy(h, peer, row).wait_send()
            gg_copy(h, peer, row).wait_send()
        for step in range(2, n_row, 2):
            b_copy(h, row_peer(step), row).wait_send()
            b_forward(h, row_peer(n_row - step)).wait_send()
        b_copy(h, partner, row).wait_send()

    @pl.when(col == root)
    def _():
        for h in range(parts):
            for step in range(1, n_col):
                w_copy(h, col_peer(step)).wait_send()


PARTS = 2


def solution(mesh):
    n_row, n_col = mesh.shape["row"], mesh.shape["col"]

    def body(front_rows, slot_blocks, inv_factor, ancestor_inv):
        _, height, width = front_rows.shape
        tile_rows, panel_rows = ancestor_inv.shape
        block_height = height * n_col
        share = tile_rows // n_col
        diag_width = width // n_col
        piece = diag_width // n_row
        parts, part_width = PARTS, width // PARTS
        wire = BF16 if piece % 16 == 0 else F32
        vmem = pltpu.VMEM

        def dma(*shape):
            return pltpu.SemaphoreType.DMA(shape)

        in_vmem = pl.BlockSpec(memory_space=pltpu.VMEM)
        anywhere = pl.BlockSpec(memory_space=pl.ANY)
        total, gram, factor_gram = pl.pallas_call(
            functools.partial(kernel, n_row, n_col, parts),
            out_shape=(
                jax.ShapeDtypeStruct((share, width), F32),
                jax.ShapeDtypeStruct((diag_width, width), F32),
                jax.ShapeDtypeStruct((diag_width, width), F32),
            ),
            in_specs=[in_vmem, pl.BlockSpec(memory_space=pltpu.SMEM), anywhere, anywhere],
            out_specs=(in_vmem, in_vmem, in_vmem),
            scratch_shapes=[
                vmem((width, width), F32),
                vmem((tile_rows, panel_rows), F32),
                vmem((n_row, 8, max(part_width, block_height)), jnp.int32),
                vmem((parts, n_col, height, part_width), BF16),
                vmem((parts, n_row, n_col, height, part_width), BF16),
                vmem((n_row, tile_rows, block_height), BF16),
                vmem((parts, tile_rows, part_width), F32),
                vmem((parts, n_col, share, part_width), BF16),
                vmem((parts, n_col, share, part_width), BF16),
                vmem((parts, share, part_width), BF16),
                vmem((parts, n_col, share, part_width), BF16),
                vmem((width, width), F32),
                vmem((parts, n_row, n_col, piece, part_width), wire),
                vmem((parts, n_row, n_col, piece, part_width), wire),
                vmem((parts, n_col, piece, part_width), F32),
                vmem((parts, n_col, piece, part_width), F32),
                vmem((parts, n_row, piece, part_width), F32),
                dma(2),
                dma(n_row), dma(n_row),
                dma(parts, n_col), dma(parts, n_col),
                dma(parts, n_row), dma(parts, n_row), dma(parts, n_row),
                dma(parts, n_col), dma(parts, n_col),
                dma(parts, n_col), dma(parts),
                dma(parts, n_row), dma(parts, n_row),
                dma(parts, n_col), dma(parts, n_col),
                dma(parts, n_row), dma(parts, n_row),
            ],
            compiler_params=pltpu.CompilerParams(
                collective_id=0, has_side_effects=True, vmem_limit_bytes=60 * 1024 * 1024
            ),
        )(front_rows, slot_blocks, inv_factor, ancestor_inv)
        return -total, factor_gram + gram

    in_specs = (P("row", "col", None), P("row"), P(), P("row", "col"))
    out_specs = (P(("row", "col"), None), P("col", None))
    return jax.shard_map(body, mesh=mesh, in_specs=in_specs, out_specs=out_specs, check_vma=False)
```

time: 56.5 us -> 51.2 us (0.906)
  Pallas kernels: 52.3 us -> 46.9 us
  other arithmetic: 0 us -> 3.39 us
  local copies, waits for them, and re-layouts: 3.29 us -> 0 us
    pallas_call x1, Pallas kernels: 52.3 us -> 46.9 us  [body(): pl.pallas_call(functools.partial(kernel, n_row, n_col, parts), out_shape=...]
    unnamed x2 -> x0, local copies, waits for them, and re-layouts: 3.29 us -> none
    add x0 -> x1, other arithmetic: none -> 1.77 us  [body(): return (-total, factor_gram + gram)]
    neg x0 -> x1, other arithmetic: none -> 1.62 us  [body(): return (-total, factor_gram + gram)]
where the time goes in v2:
time: 51.2 us; the launch traced here: 51 us
  Pallas kernels  46.9 us (92%)
  other arithmetic  3.39 us (7%)
  between operations  0.64 us (1%)
    pallas_call x1, Pallas kernels, body(): pl.pallas_call(functools.partial(kernel, n_row, n_col, parts), out_shape=...  46.9 us
    add x1, other arithmetic, body(): return (-total, factor_gram + gram)  1.77 us
    neg x1, other arithmetic, body(): return (-total, factor_gram + gram)  1.62 us

profile of v2, /device:TPU:0, one launch (start us, length us, event | category | flops | bytes accessed | tf_op | source)
XLA Modules:
  0.0 51.0 jit_solution(10398225226649217728)
XLA Ops:
  0.6 46.9 %shard_map.59 = (f32[96,512]{1,0:T(8,128)}, f32[128,512]{1,0:T(8,128)}, f32[128,512]{1,0:T(8,128)}) custom-call(bf16[4,32,512]{2,1,0:T(8,128)(2,1)} %front.1, s32[4]{0:T(128)} %slots.1, f32[512,512]{1,0:T(8,128)} %factor_hbm.1, f32[384,768]{1,0:T(8,128)} %anc_hbm.1), custom_call_target="tpu_custom_call" | custom-call | tf_op jit(solution)/shard_map/pallas_call | solution.py:313
  47.6 1.6 %neg.3 = f32[96,512]{1,0:T(8,128)} negate(f32[96,512]{1,0:T(8,128)} %get-tuple-element.5) | non-fusion elementwise | flops 49152 | bytes 393216 | tf_op jit(solution)/shard_map/neg | solution.py:354
  49.2 1.8 %add.3 = f32[128,512]{1,0:T(8,128)} add(f32[128,512]{1,0:T(8,128)} %get-tuple-element.6, f32[128,512]{1,0:T(8,128)} %get-tuple-element.7) | non-fusion elementwise | flops 65536 | bytes 786432 | tf_op jit(solution)/shard_map/add | solution.py:354

commit v3 on v2

--- a/solution.py
+++ b/solution.py
@@ -42,6 +42,10 @@
     piece = row_out.shape[3]
     part_width = width // parts
     partner = row + 1 - 2 * lax.rem(row, 2)
+    half = n_row // 2
+
+    def place(m):
+        return lax.rem(m, 2) * half + m // 2
 
     def row_peer(step):
         return lax.rem(row + step, n_row)
@@ -88,12 +92,12 @@
         for p in range(n_col):
             piece_rows = scaled[p * height:(p + 1) * height, h * part_width:(h + 1) * part_width]
             pieces[h, p] = piece_rows.astype(BF16)
-        blocks[h, row, col] = pieces[h, col]
+        blocks[h, place(row), col] = pieces[h, col]
     pl.semaphore_wait(barrier, n_row + n_col - 2)
 
     def a_copy(h, peer, there):
         return copy(
-            pieces.at[h, peer], blocks.at[h, row, there], a_s.at[h, peer], a_r.at[h, there], row, peer
+            pieces.at[h, peer], blocks.at[h, place(row), there], a_s.at[h, peer], a_r.at[h, there], row, peer
         )
 
     def id_copy(peer, there):
@@ -108,12 +112,12 @@
 
     def b_copy(h, peer, there):
         return copy(
-            blocks.at[h, there], blocks.at[h, there], b_s.at[h, peer], b_r.at[h, there], peer, col
+            blocks.at[h, place(there)], blocks.at[h, place(there)], b_s.at[h, peer], b_r.at[h, there], peer, col
         )
 
     def b_forward(h, there):
         return copy(
-            blocks.at[h, there], blocks.at[h, there], f_s.at[h, there], b_r.at[h, there], partner, col
+            blocks.at[h, place(there)], blocks.at[h, place(there)], f_s.at[h, there], b_r.at[h, there], partner, col
         )
 
     for h in range(parts):
@@ -127,19 +131,25 @@
         id_copy(row_peer(step), row_peer(step)).wait_recv()
     load_anc.wait()
 
-    @pl.loop(0, n_row)
-    def _(m):
-        mask_ids = ids[m, 0:1, 0:block_height]
-        total = jnp.zeros((tile_rows, block_height), F32)
-        for b in range(panel_blocks):
-            keep = jnp.where(mask_ids == b, 1.0, 0.0)
-            total = total + anc[:, b * block_height:(b + 1) * block_height] * keep
-        perm[m] = total.astype(BF16)
-
-    def block_of(h, m):
+    for side in range(2):
+        @pl.loop(0, half)
+        def _(q):
+            mask_ids = ids[2 * q + side, 0:1, 0:block_height]
+            total = jnp.zeros((tile_rows, block_height), F32)
+            for b in range(panel_blocks):
+                keep = jnp.where(mask_ids == b, 1.0, 0.0)
+                total = total + anc[:, b * block_height:(b + 1) * block_height] * keep
+            lanes = pl.ds(pl.multiple_of(q * block_height, block_height), block_height)
+            perm[side, :, lanes] = total.astype(BF16)
+
+    def block_of(h, m, count=1):
+        held = blocks[h, pl.ds(m, count)]
         if height % 16 == 0:
-            return blocks[h, m].reshape(block_height, part_width)
-        return blocks[h, m].astype(F32).reshape(block_height, part_width).astype(BF16)
+            return held.reshape(count * block_height, part_width)
+        return held.astype(F32).reshape(count * block_height, part_width).astype(BF16)
+
+    def half_product(h, side):
+        return dot(perm[side], block_of(h, side * half, half))
 
     root = row * n_col // n_row
     first = (row * tile_rows - root * panel_rows) // block_height
@@ -166,7 +176,7 @@
                 chosen = jnp.zeros((block_height, part_width), F32)
                 for m in range(n_row):
                     keep = jnp.where(ids[m, 0:1, 0:part_width] == first + i, 1.0, 0.0)
-                    chosen = chosen + block_of(h, m).astype(F32) * keep
+                    chosen = chosen + block_of(h, (m % 2) * half + m // 2).astype(F32) * keep
                 rows.append(chosen)
             rows = jnp.concatenate(rows, axis=0)
             for p in range(n_col):
@@ -176,16 +186,15 @@
             own_rows[h] = spread[h, col]
 
     for h in range(parts):
-        acc[h] = dot(perm[row], block_of(h, row))
         for step in range(2, n_row, 2):
             m = row_peer(n_row - step)
             b_copy(h, m, m).wait_recv()
             b_forward(h, m).start()
-            acc[h] += dot(perm[m], block_of(h, m))
+        acc[h] = half_product(h, lax.rem(row, 2))
         for step in range(0, n_row, 2):
             m = lax.rem(partner + n_row - step, n_row)
             b_copy(h, m, m).wait_recv()
-            acc[h] += dot(perm[m], block_of(h, m))
+        acc[h] += half_product(h, lax.rem(partner, 2))
         if h < parts - 1:
             send_sums(h)
             send_rows(h)
@@ -313,9 +322,9 @@
         total, gram, factor_gram = pl.pallas_call(
             functools.partial(kernel, n_row, n_col, parts),
             out_shape=(
-                jax.ShapeDtypeStruct((share, width), F32),
-                jax.ShapeDtypeStruct((diag_width, width), F32),
-                jax.ShapeDtypeStruct((diag_width, width), F32),
+                pltpu.VMEM((share, width), F32),
+                pltpu.VMEM((diag_width, width), F32),
+                pltpu.VMEM((diag_width, width), F32),
             ),
             in_specs=[in_vmem, pl.BlockSpec(memory_space=pltpu.SMEM), anywhere, anywhere],
             out_specs=(in_vmem, in_vmem, in_vmem),
@@ -325,7 +334,7 @@
                 vmem((n_row, 8, max(part_width, block_height)), jnp.int32),
                 vmem((parts, n_col, height, part_width), BF16),
                 vmem((parts, n_row, n_col, height, part_width), BF16),
-                vmem((n_row, tile_rows, block_height), BF16),
+                vmem((2, tile_rows, n_row // 2 * block_height), BF16),
                 vmem((parts, tile_rows, part_width), F32),
                 vmem((parts, n_col, share, part_width), BF16),
                 vmem((parts, n_col, share, part_width), BF16),

time: 51.2 us -> 48.1 us (0.939)
  other arithmetic: 3.39 us -> 1.43 us
  Pallas kernels: 46.9 us -> 45.9 us
    pallas_call x1, Pallas kernels: 46.9 us -> 45.9 us  [body(): pl.pallas_call(functools.partial(kernel, n_row, n_col, parts), out_shape=...]
    add x1, other arithmetic: 1.77 us -> 0.74 us  [body(): return (-total, factor_gram + gram)]
    neg x1, other arithmetic: 1.62 us -> 0.69 us  [body(): return (-total, factor_gram + gram)]
where the time goes in v3:
time: 48.1 us; the launch traced here: 47.9 us
  Pallas kernels  45.9 us (95%)
  other arithmetic  1.43 us (3%)
  between operations  0.64 us (1%)
    pallas_call x1, Pallas kernels, body(): pl.pallas_call(functools.partial(kernel, n_row, n_col, parts), out_shape=...  45.9 us

profile of v3, /device:TPU:0, one launch (start us, length us, event | category | flops | bytes accessed | tf_op | source)
XLA Modules:
  0.0 47.9 jit_solution(10345953309940231071)
XLA Ops:
  0.6 45.9 %shard_map.59 = (f32[96,512]{1,0:T(8,128)S(1)}, f32[128,512]{1,0:T(8,128)S(1)}, f32[128,512]{1,0:T(8,128)S(1)}) custom-call(bf16[4,32,512]{2,1,0:T(8,128)(2,1)} %front.1, s32[4]{0:T(128)} %slots.1, f32[512,512]{1,0:T(8,128)} %factor_hbm.1, f32[384,768]{1,0:T(8,128)} %anc_hbm.1), custom_call_target="tpu_custom_call" | custom-call | tf_op jit(solution)/shard_map/pallas_call | solution.py:322
  46.5 0.7 %neg.3 = f32[96,512]{1,0:T(8,128)} negate(f32[96,512]{1,0:T(8,128)S(1)} %get-tuple-element.5) | non-fusion elementwise | flops 49152 | bytes 393216 | tf_op jit(solution)/shard_map/neg | solution.py:363
  47.2 0.7 %add.3 = f32[128,512]{1,0:T(8,128)} add(f32[128,512]{1,0:T(8,128)S(1)} %get-tuple-element.6, f32[128,512]{1,0:T(8,128)S(1)} %get-tuple-element.7) | non-fusion elementwise | flops 65536 | bytes 786432 | tf_op jit(solution)/shard_map/add | solution.py:363

commit v4 on v3

--- a/solution.py
+++ b/solution.py
@@ -28,7 +28,7 @@
 def kernel(
     n_row, n_col, parts, front, slots, factor_hbm, anc_hbm, out, diag, fdiag,
     factor, anc, ids, pieces, blocks, perm, acc, part, part_in, own_rows, spread,
-    gram, row_out, row_in, col_out, col_in, total_in,
+    spare, gram, row_out, row_in, col_out, col_in, total_in,
     load_sem, ids_s, ids_r, a_s, a_r, b_s, b_r, f_s, c_s, c_r, w_s, w_r,
     gr_s, gr_r, gc_s, gc_r, gg_s, gg_r,
 ):
@@ -64,6 +64,14 @@
         pl.semaphore_signal(barrier, inc=1, device_id=(row_peer(step), col), device_id_type=MESH)
     for step in range(1, n_col):
         pl.semaphore_signal(barrier, inc=1, device_id=(row, col_peer(step)), device_id_type=MESH)
+    across = lax.rem(row + n_row // 2, n_row)
+    own_root = row * n_col // n_row
+    across_root = across * n_col // n_row
+
+    @pl.when(col != own_root)
+    def _():
+        pl.semaphore_signal(barrier, inc=1, device_id=(across, own_root), device_id_type=MESH)
+
     load_factor = pltpu.make_async_copy(factor_hbm, factor, load_sem.at[0])
     load_anc = pltpu.make_async_copy(anc_hbm, anc, load_sem.at[1])
     load_factor.start()
@@ -93,7 +101,8 @@
             piece_rows = scaled[p * height:(p + 1) * height, h * part_width:(h + 1) * part_width]
             pieces[h, p] = piece_rows.astype(BF16)
         blocks[h, place(row), col] = pieces[h, col]
-    pl.semaphore_wait(barrier, n_row + n_col - 2)
+    extra = jnp.where(col == across_root, n_col - 1, 0)
+    pl.semaphore_wait(barrier, n_row + n_col - 2 + extra)
 
     def a_copy(h, peer, there):
         return copy(
@@ -160,7 +169,7 @@
         )
 
     def w_copy(h, peer):
-        return copy(spread.at[h, peer], own_rows.at[h], w_s.at[h, peer], w_r.at[h], row, peer)
+        return copy(spread.at[h, peer], own_rows.at[h], w_s.at[h, peer], w_r.at[h], lax.rem(row + (n_row // 2) * (h % 2), n_row), peer)
 
     def send_sums(h):
         for p in range(n_col):
@@ -169,20 +178,38 @@
             c_copy(h, col_peer(n_col - step), col).start()
 
     def send_rows(h):
+        away = n_row // 2 if h % 2 == 1 else 0
+        target = lax.rem(row + away, n_row)
+        goal = target * n_col // n_row
+        begin = (target * tile_rows - goal * panel_rows) // block_height
+
         @pl.when(col == root)
         def _():
-            rows = []
-            for i in range(tile_rows // block_height):
-                chosen = jnp.zeros((block_height, part_width), F32)
-                for m in range(n_row):
-                    keep = jnp.where(ids[m, 0:1, 0:part_width] == first + i, 1.0, 0.0)
-                    chosen = chosen + block_of(h, (m % 2) * half + m // 2).astype(F32) * keep
-                rows.append(chosen)
-            rows = jnp.concatenate(rows, axis=0)
-            for p in range(n_col):
-                spread[h, p] = rows[p * share:(p + 1) * share].astype(BF16)
-            for step in range(1, n_col):
-                w_copy(h, col_peer(step)).start()
+            if away:
+                build(h, row, root, first, False)
+
+        @pl.when(col == goal)
+        def _():
+            build(h, target, goal, begin, True)
+
+    def build(h, target, goal, begin, send):
+        rows = []
+        for i in range(tile_rows // block_height):
+            chosen = jnp.zeros((block_height, part_width), F32)
+            for m in range(n_row):
+                keep = jnp.where(ids[m, 0:1, 0:part_width] == begin + i, 1.0, 0.0)
+                chosen = chosen + block_of(h, (m % 2) * half + m // 2).astype(F32) * keep
+            rows.append(chosen)
+        rows = jnp.concatenate(rows, axis=0)
+        if not send:
+            spare[...] = rows
+            own_rows[h] = spare[pl.ds(pl.multiple_of(col * share, 8), share), :].astype(BF16)
+            return
+        for p in range(n_col):
+            spread[h, p] = rows[p * share:(p + 1) * share].astype(BF16)
+        for step in range(1, n_col):
+            w_copy(h, col_peer(step)).start()
+        if h % 2 == 0:
             own_rows[h] = spread[h, col]
 
     for h in range(parts):
@@ -293,6 +320,13 @@
     @pl.when(col == root)
     def _():
         for h in range(parts):
+            for step in range(1, n_col):
+                pass
+    for h in range(parts):
+        goal = lax.rem(row + (n_row // 2) * (h % 2), n_row) * n_col // n_row
+
+        @pl.when(col == goal)
+        def _():
             for step in range(1, n_col):
                 w_copy(h, col_peer(step)).wait_send()
 
@@ -340,6 +374,7 @@
                 vmem((parts, n_col, share, part_width), BF16),
                 vmem((parts, share, part_width), BF16),
                 vmem((parts, n_col, share, part_width), BF16),
+                vmem((tile_rows, part_width), F32),
                 vmem((width, width), F32),
                 vmem((parts, n_row, n_col, piece, part_width), wire),
                 vmem((parts, n_row, n_col, piece, part_width), wire),

time: 48.1 us -> 47.2 us (0.981)
  Pallas kernels: 45.9 us -> 45 us
    pallas_call x1, Pallas kernels: 45.9 us -> 45 us  [body(): pl.pallas_call(functools.partial(kernel, n_row, n_col, parts), out_shape=...]
where the time goes in v4:
time: 47.2 us; the launch traced here: 47 us
  Pallas kernels  45 us (95%)
  other arithmetic  1.43 us (3%)
  between operations  0.64 us (1%)
    pallas_call x1, Pallas kernels, body(): pl.pallas_call(functools.partial(kernel, n_row, n_col, parts), out_shape=...  45 us

profile of v4, /device:TPU:0, one launch (start us, length us, event | category | flops | bytes accessed | tf_op | source)
XLA Modules:
  0.0 47.0 jit_solution(15549155944340034498)
XLA Ops:
  0.6 45.0 %shard_map.59 = (f32[96,512]{1,0:T(8,128)S(1)}, f32[128,512]{1,0:T(8,128)S(1)}, f32[128,512]{1,0:T(8,128)S(1)}) custom-call(bf16[4,32,512]{2,1,0:T(8,128)(2,1)} %front.1, s32[4]{0:T(128)} %slots.1, f32[512,512]{1,0:T(8,128)} %factor_hbm.1, f32[384,768]{1,0:T(8,128)} %anc_hbm.1), custom_call_target="tpu_custom_call" | custom-call | tf_op jit(solution)/shard_map/pallas_call | solution.py:356
  45.6 0.7 %neg.3 = f32[96,512]{1,0:T(8,128)} negate(f32[96,512]{1,0:T(8,128)S(1)} %get-tuple-element.5) | non-fusion elementwise | flops 49152 | bytes 393216 | tf_op jit(solution)/shard_map/neg | solution.py:398
  46.3 0.7 %add.3 = f32[128,512]{1,0:T(8,128)} add(f32[128,512]{1,0:T(8,128)S(1)} %get-tuple-element.6, f32[128,512]{1,0:T(8,128)S(1)} %get-tuple-element.7) | non-fusion elementwise | flops 65536 | bytes 786432 | tf_op jit(solution)/shard_map/add | solution.py:398
